TPU v7x, 256 devices: a whole 4x4x8 slice. The times are simulated.
256 devices in a mesh: grp: 8 (over z), ord: 32 (over x, y, core).
Axes of the slice: x: 4, y: 4, z: 8, core: 2. Of those that a mesh axis runs over, the one named last changes fastest.
Arguments:
- legendre: float32 [512, 1048576], P('ord', 'grp')
- lon_center: float32 [8], P('grp'), may hold values from 0 to 1
- counts: int32 [8, 32], P('grp'), may hold values from 1 to 4096, 98304 in all within a row
- column_index: int32 [3, 512], replicated, may hold values from 0 to 120, as said below
Outputs:
- factor: float32 [512, 512], replicated
Inputs may be any that keep to these rules, and one draw needn't show every extreme that they name: `column_index`: each column names a different coefficient: row 0 is its degree (at most 120), row 1 its order (at most the degree), row 2 is 1 for a sine term and 0 for a cosine term, and 0 at order 0. Each group's counts add up to 98304.
All inputs are finite; a program needn't handle non-finite values.
Results may differ from a plain program's by a relative error of at most 0.0003.
Values sent between devices are 32-bit elements; how exact they have to be, the bound alone decides.
A program may use at most 64 MiB of HBM per device.

v0:
```python
import math
import jax
import jax.numpy as jnp
from jax import lax
from jax.sharding import PartitionSpec as P

NMAX = 120
quarter_turn = math.pi / 2
track_span = 0.3
kaula_gain = 1.2
highest = lax.Precision.HIGHEST


def upper_factor(matrix):
    return jnp.linalg.cholesky(matrix).T


def block_grams(exchanged):
    blocks = exchanged[:, 0]
    return jnp.einsum("jkb,lkb->kjl", blocks, blocks, precision=highest)


def body(legendre, lon_center, counts, column_index):
    ord_size = lax.axis_size("ord")
    grp_size = lax.axis_size("grp")
    cols_dev, rows_grp = legendre.shape
    rows_dev = rows_grp // ord_size
    scaling = 1.0 / math.sqrt(rows_grp * grp_size)
    own_columns = lax.dynamic_slice_in_dim(
        column_index, lax.axis_index("ord") * cols_dev, cols_dev, 1
    )
    harmonic = own_columns[1].astype(jnp.float32)
    sine_part = own_columns[2].astype(jnp.float32)
    longitude = lon_center[0] + jnp.arange(rows_grp, dtype=jnp.float32) * (track_span / rows_grp)
    harmonic_wave = jnp.cos(
        harmonic[:, None] * longitude[None, :] - sine_part[:, None] * quarter_turn
    )
    slot_index = jnp.arange(rows_dev, dtype=jnp.int32)
    row_valid = (slot_index[None, :] < counts[0][:, None]).astype(jnp.float32).reshape(rows_grp)
    design = legendre * harmonic_wave * (row_valid * scaling)[None, :]
    block_rows = min(512, rows_dev)
    shaped = design.reshape(cols_dev, ord_size, rows_dev // block_rows, block_rows)
    block_gram = block_grams(lax.all_to_all(shaped, "ord", split_axis=1, concat_axis=0, tiled=True))
    local_gram = jnp.sum(block_gram, axis=0)
    degree = column_index[0].astype(jnp.float32)
    kaula_weight = kaula_gain * (degree / NMAX) ** 2
    regular = jnp.diag(kaula_weight * kaula_weight)
    normal = lax.psum(local_gram, ("grp", "ord")) + regular
    return upper_factor(normal)


def solution(mesh):
    placed = (P("ord", "grp"), P("grp"), P("grp", None), P())
    return jax.shard_map(body, mesh=mesh, in_specs=placed, out_specs=P(), check_vma=False)
```

profile of v0, /device:TPU:2, one launch (start us, length us, event | category | flops | bytes accessed | tf_op | source)
XLA Modules:
  0.0 538.6 jit_solution(2535784197587066006)
XLA Ops:
  6.5 0.8 constant_dynamic-slice_fusion
  7.3 0.8 select_bitcast_fusion.1
  9.0 29.6 %multiply_multiply_fusion = f32[16,131072]{1,0:T(8,128)S(1)} fusion(f32[16,131072]{1,0:T(8,128)} %param.4, f32[131072]{0:T(1024)S(1)} %bitcast.48, f32[16]{0:T(128)S(1)} %multiply_bitcast_fusion, f32[131072]{0:T(1024)S(1)} %multiply_add_fusion, f32[16]{0:T(128)S(1)} %convert_bitcast_fusion), kind=kLoop, calls=%fused_computation | loop fusion | flops 8388608 | bytes 17825920 | tf_op jit(solution)/shard_map/mul | solution.py:40
  38.6 4.9 copy.41
  43.5 20.4 %copy.25 = f32[16,32,8,512]{3,0,2,1:T(8,128)S(1)} copy(f32[16,32,8,512]{3,2,1,0:T(8,128)S(1)} %bitcast.46) | data formatting | bytes 16777216 | tf_op jit(solution)/shard_map/reshape | solution.py:42
  63.8 100.5 %all_to_all.15 = f32[16,32,8,512]{3,0,2,1:T(8,128)S(1)} all-to-all(f32[16,32,8,512]{3,0,2,1:T(8,128)S(1)} %copy.25), channel_id=1, replica_groups=mesh['grp'=8,'ord'=32] {'ord'}, dimensions={1} | all-to-all | bytes 16777216 | tf_op jit(solution)/shard_map/all_to_all | solution.py:43
  164.3 1.9 copy.26
  166.2 16.1 %convolution_bitcast_fusion = f32[512,512]{0,1:T(8,128)} fusion(f32[512,8,512]{2,0,1:T(8,128)S(1)} %bitcast.44), kind=kOutput, calls=%fused_computation.1 | convolution fusion | flops 12884901888 | bytes 9437184 | tf_op jit(solution)/shard_map/jkb,lkb->kjl/dot_general | solution.py:20
  182.4 0.7 multiply_multiply_fusion.1
  183.1 259.9 %all-reduce.3.cloned.1.call-done = f32[512,512]{0,1:T(8,128)} async-done(((f32[512,512]{0,1:T(8,128)}), f32[512,512]{0,1:T(8,128)}) %all-reduce.3.cloned.1.call-update) | async-done | bytes 1048592 | tf_op jit(solution)/shard_map/psum | solution.py:48
  443.0 1.3 select_add_fusion
  444.7 1.4 fusion
  446.1 11.7 %cholesky.103 = f32[128,128]{1,0:T(8,128)S(1)} custom-call(f32[128,128]{1,0:T(8,128)S(1)} %cholesky.263), custom_call_target="Cholesky" | custom-call | tf_op jit(solution)/shard_map/jit(cholesky)/cholesky | solution.py:15
  457.9 9.8 %custom-call.27 = f32[1,128,128]{1,2,0:T(8,128)S(1)} custom-call(f32[1,128,128]{2,1,0:T(8,128)S(1)} %get-tuple-element.10), custom_call_target="InvertDiagBlocksLowerTriangular" | custom-call | tf_op jit(solution)/shard_map/jit(cholesky)/cholesky | solution.py:15
  468.4 11.7 %cholesky.215 = f32[128,128]{1,0:T(8,128)S(1)} custom-call(f32[128,128]{1,0:T(8,128)S(1)} %cholesky.267), custom_call_target="Cholesky" | custom-call | tf_op jit(solution)/shard_map/jit(cholesky)/cholesky | solution.py:15
  480.5 9.9 %custom-call.28 = f32[1,128,128]{1,2,0:T(8,128)S(1)} custom-call(f32[1,128,128]{2,1,0:T(8,128)S(1)} %get-tuple-element.8), custom_call_target="InvertDiagBlocksLowerTriangular" | custom-call | tf_op jit(solution)/shard_map/jit(cholesky)/cholesky | solution.py:15
  490.9 0.6 convolution_subtract_fusion.1
  491.5 11.7 %cholesky.236 = f32[128,128]{1,0:T(8,128)S(1)} custom-call(f32[128,128]{1,0:T(8,128)S(1)} %cholesky.272), custom_call_target="Cholesky" | custom-call | tf_op jit(solution)/shard_map/jit(cholesky)/cholesky | solution.py:15
  503.4 9.8 %custom-call.29 = f32[1,128,128]{1,2,0:T(8,128)S(1)} custom-call(f32[1,128,128]{2,1,0:T(8,128)S(1)} %get-tuple-element.6), custom_call_target="InvertDiagBlocksLowerTriangular" | custom-call | tf_op jit(solution)/shard_map/jit(cholesky)/cholesky | solution.py:15
  514.0 11.7 %cholesky.253 = f32[128,128]{1,0:T(8,128)S(1)} custom-call(f32[128,128]{1,0:T(8,128)S(1)} %convolution_subtract_fusion.2), custom_call_target="Cholesky" | custom-call | tf_op jit(solution)/shard_map/jit(cholesky)/cholesky | solution.py:15
  525.8 0.7 compare_reduce_fusion.1
  526.5 0.6 compare_reduce_fusion
  527.2 0.7 compare_reduce_fusion.2
  530.4 1.1 select_bitcast_fusion
  (29 shorter events, 3.2 us)
Async XLA Ops:
  6.5 436.4 %all-reduce.3.cloned.1.call-start = ((), (), s32[]{:S(2)}) async-start(), calls=%async_computation.1 | async-start | bytes 2097152 | tf_op jit(solution)/shard_map/psum | solution.py:48
Sparse Core Ops, SparseCore 0:
  182.5 260.4 all-reduce.2
where the time goes:
time: 542 us; the launch traced here: 539 us
  waiting for transfers between devices  260 us (48%)
  other arithmetic  114 us (21%)
  blocking collectives  100 us (18%)
  local copies, waits for them, and re-layouts  29 us (5%)
  matrix products  18.5 us (3%)
  between operations  17 us (3%)
    psum x1, waiting for transfers between devices, body(): normal = lax.psum(local_gram, ('grp', 'ord')) + regular  260 us
    all_to_all x1, blocking collectives, body(): lax.all_to_all(shaped, 'ord', split_axis=1, concat_axis=0, tiled=True)  100 us
    another operation x14, other arithmetic, upper_factor(): return jnp.linalg.cholesky(matrix).T  78.6 us
    mul x1, other arithmetic, body(): design = legendre * harmonic_wave * (row_valid * scaling)[None, :]  29.6 us
    reshape x1, local copies, waits for them, and re-layouts, body(): design.reshape(cols_dev, ord_size, rows_dev // block_rows, block_rows)  20.4 us
    dot_general x1, matrix products, block_grams(): return jnp.einsum('jkb,lkb->kjl', blocks, blocks, precision=highest)  16.1 us
  transfers between devices with their start and end apart: 1, of which 1 were waited for; matrix products, arithmetic and copies ran while one was open for 0% of the time, Pallas kernels for 0%

commit v1 on v0

--- a/solution.py
+++ b/solution.py
@@ -1,3 +1,4 @@
+import functools
 import math
 import jax
 import jax.numpy as jnp
@@ -9,6 +10,15 @@
 track_span = 0.3
 kaula_gain = 1.2
 highest = lax.Precision.HIGHEST
+
+
+def open_cards(row_data, shard_axis, mesh_dim):
+    for pp in (shard_axis, mesh_dim):
+        row_data = lax.psum(row_data, pp)
+    return row_data
+
+
+search_digits_on = functools.partial(open_cards, shard_axis="ord", mesh_dim="grp")
 
 
 def upper_factor(matrix):
@@ -45,7 +55,7 @@
     degree = column_index[0].astype(jnp.float32)
     kaula_weight = kaula_gain * (degree / NMAX) ** 2
     regular = jnp.diag(kaula_weight * kaula_weight)
-    normal = lax.psum(local_gram, ("grp", "ord")) + regular
+    normal = search_digits_on(local_gram) + regular
     return upper_factor(normal)
 
 

time: 542 us -> 477 us (0.88)
  waiting for transfers between devices: 260 us -> 195 us
    psum x1 -> x2, waiting for transfers between devices: 260 us -> 195 us  [open_cards(): row_data = lax.psum(row_data, pp)]
  transfers between devices with their start and end apart: 1 -> 2, of which waited for: 1 -> 2; matrix products, arithmetic and copies ran while one was open for 0% -> 0% of each run, Pallas kernels for 0% -> 0%
where the time goes in v1:
time: 477 us; the launch traced here: 473 us
  waiting for transfers between devices  195 us (41%)
  other arithmetic  114 us (24%)
  blocking collectives  100 us (21%)
  local copies, waits for them, and re-layouts  29 us (6%)
  matrix products  18.5 us (4%)
  between operations  17 us (4%)
    psum x2, waiting for transfers between devices, open_cards(): row_data = lax.psum(row_data, pp)  195 us
    all_to_all x1, blocking collectives, body(): lax.all_to_all(shaped, 'ord', split_axis=1, concat_axis=0, tiled=True)  100 us
    another operation x14, other arithmetic, upper_factor(): return jnp.linalg.cholesky(matrix).T  78.6 us
    mul x1, other arithmetic, body(): design = legendre * harmonic_wave * (row_valid * scaling)[None, :]  29.6 us
    reshape x1, local copies, waits for them, and re-layouts, body(): design.reshape(cols_dev, ord_size, rows_dev // block_rows, block_rows)  20.4 us
    dot_general x1, matrix products, block_grams(): return jnp.einsum('jkb,lkb->kjl', blocks, blocks, precision=highest)  16.1 us
  transfers between devices with their start and end apart: 2, of which 2 were waited for; matrix products, arithmetic and copies ran while one was open for 0% of the time, Pallas kernels for 0%

profile of v1, /device:TPU:2, one launch (start us, length us, event | category | flops | bytes accessed | tf_op | source)
XLA Modules:
  0.0 473.4 jit_solution(15740051857572074123)
XLA Ops:
  6.5 0.8 constant_dynamic-slice_fusion
  7.3 0.8 select_bitcast_fusion.1
  9.0 29.6 %multiply_multiply_fusion = f32[16,131072]{1,0:T(8,128)S(1)} fusion(f32[16,131072]{1,0:T(8,128)} %param.4, f32[131072]{0:T(1024)S(1)} %bitcast.48, f32[16]{0:T(128)S(1)} %multiply_bitcast_fusion, f32[131072]{0:T(1024)S(1)} %multiply_add_fusion, f32[16]{0:T(128)S(1)} %convert_bitcast_fusion), kind=kLoop, calls=%fused_computation | loop fusion | flops 8388608 | bytes 17825920 | tf_op jit(solution)/shard_map/mul | solution.py:50
  38.6 4.9 %copy.41 = f32[2,8,256,512]{3,2,1,0:T(8,128)S(1)} copy(f32[2,8,256,512]{3,1,2,0:T(8,128)S(1)} %bitcast.45) | data formatting | bytes 16777216
  43.5 20.4 %copy.25 = f32[16,32,8,512]{3,0,2,1:T(8,128)S(1)} copy(f32[16,32,8,512]{3,2,1,0:T(8,128)S(1)} %bitcast.46) | data formatting | bytes 16777216 | tf_op jit(solution)/shard_map/reshape | solution.py:52
  63.9 100.5 %all_to_all.15 = f32[16,32,8,512]{3,0,2,1:T(8,128)S(1)} all-to-all(f32[16,32,8,512]{3,0,2,1:T(8,128)S(1)} %copy.25), channel_id=1, replica_groups=mesh['grp'=8,'ord'=32] {'ord'}, dimensions={1} | all-to-all | bytes 16777216 | tf_op jit(solution)/shard_map/all_to_all | solution.py:53
  164.3 1.9 copy.26
  166.3 16.1 %convolution_bitcast_fusion = f32[512,512]{0,1:T(8,128)} fusion(f32[512,8,512]{2,0,1:T(8,128)S(1)} %bitcast.44), kind=kOutput, calls=%fused_computation.1 | convolution fusion | flops 12884901888 | bytes 9437184 | tf_op jit(solution)/shard_map/jkb,lkb->kjl/dot_general | solution.py:30
  182.5 116.7 %all-reduce.4.cloned.1.call-done = f32[512,512]{0,1:T(8,128)} async-done(((f32[512,512]{0,1:T(8,128)}), f32[512,512]{0,1:T(8,128)}) %all-reduce.4.cloned.1.call-update) | async-done | bytes 1048592 | tf_op jit(solution)/shard_map/psum | solution.py:17
  299.1 0.7 multiply_multiply_fusion.1
  299.8 78.0 %all-reduce.6.cloned.1.call-done = f32[512,512]{0,1:T(8,128)} async-done(((f32[512,512]{0,1:T(8,128)}), f32[512,512]{0,1:T(8,128)}) %all-reduce.6.cloned.1.call-update) | async-done | bytes 1048592 | tf_op jit(solution)/shard_map/psum | solution.py:17
  377.8 1.3 select_add_fusion
  379.5 1.4 fusion
  381.0 11.7 %cholesky.103 = f32[128,128]{1,0:T(8,128)S(1)} custom-call(f32[128,128]{1,0:T(8,128)S(1)} %cholesky.263), custom_call_target="Cholesky" | custom-call | tf_op jit(solution)/shard_map/jit(cholesky)/cholesky | solution.py:25
  392.7 9.8 %custom-call.27 = f32[1,128,128]{1,2,0:T(8,128)S(1)} custom-call(f32[1,128,128]{2,1,0:T(8,128)S(1)} %get-tuple-element.10), custom_call_target="InvertDiagBlocksLowerTriangular" | custom-call | tf_op jit(solution)/shard_map/jit(cholesky)/cholesky | solution.py:25
  403.2 11.7 %cholesky.215 = f32[128,128]{1,0:T(8,128)S(1)} custom-call(f32[128,128]{1,0:T(8,128)S(1)} %cholesky.267), custom_call_target="Cholesky" | custom-call | tf_op jit(solution)/shard_map/jit(cholesky)/cholesky | solution.py:25
  415.3 10.0 %custom-call.28 = f32[1,128,128]{1,2,0:T(8,128)S(1)} custom-call(f32[1,128,128]{2,1,0:T(8,128)S(1)} %get-tuple-element.8), custom_call_target="InvertDiagBlocksLowerTriangular" | custom-call | tf_op jit(solution)/shard_map/jit(cholesky)/cholesky | solution.py:25
  426.4 11.7 %cholesky.236 = f32[128,128]{1,0:T(8,128)S(1)} custom-call(f32[128,128]{1,0:T(8,128)S(1)} %cholesky.272), custom_call_target="Cholesky" | custom-call | tf_op jit(solution)/shard_map/jit(cholesky)/cholesky | solution.py:25
  438.2 9.8 %custom-call.29 = f32[1,128,128]{1,2,0:T(8,128)S(1)} custom-call(f32[1,128,128]{2,1,0:T(8,128)S(1)} %get-tuple-element.6), custom_call_target="InvertDiagBlocksLowerTriangular" | custom-call | tf_op jit(solution)/shard_map/jit(cholesky)/cholesky | solution.py:25
  448.8 11.7 %cholesky.253 = f32[128,128]{1,0:T(8,128)S(1)} custom-call(f32[128,128]{1,0:T(8,128)S(1)} %convolution_subtract_fusion.2), custom_call_target="Cholesky" | custom-call | tf_op jit(solution)/shard_map/jit(cholesky)/cholesky | solution.py:25
  460.7 0.7 compare_reduce_fusion.1
  461.4 0.6 compare_reduce_fusion
  462.0 0.7 compare_reduce_fusion.2
  465.2 1.1 select_bitcast_fusion
  (32 shorter events, 3.8 us)
Async XLA Ops:
  6.5 292.6 %all-reduce.4.cloned.1.call-start = ((), (), s32[]{:S(2)}) async-start(), calls=%async_computation.1 | async-start | bytes 2097152 | tf_op jit(solution)/shard_map/psum | solution.py:17
  182.4 195.4 %all-reduce.6.cloned.1.call-start = ((), (), s32[]{:S(2)}) async-start(), calls=%async_computation.2 | async-start | bytes 2097152 | tf_op jit(solution)/shard_map/psum | solution.py:17
Sparse Core Ops, SparseCore 0:
  182.5 116.5 all-reduce.3
  301.5 76.3 all-reduce.5
